TPU v7x, 256 devices: a whole 4x4x8 slice. The times are simulated.
256 devices in a mesh: freq: 8 (over y, z_hi), dom: 32 (over x, z_lo, core).
Axes of the slice: x: 4, y: 4, z: 8 (z_hi: 2, z_lo: 4; z = z_hi * 4 + z_lo), core: 2. Of those that a mesh axis runs over, the one named last changes fastest.
Arguments:
- fwd_source: float32 [16, 4, 1024, 128], P('freq', None, 'dom'), may hold values from -6 to 6
- adj_source: float32 [16, 4, 1024, 128], P('freq', None, 'dom'), may hold values from -6 to 6
- curl_blocks: float32 [1024, 4, 128, 128], P('dom')
- block_links: int32 [1024, 4], P('dom'), may hold values from 0 to 95, as said below
- tile_lists: int32 [128, 16], P('dom'), may hold values from 0 to 31, as said below
- edge_mass: float32 [1024, 128], P('dom'), may hold values from 0.5 to 1.5
- omega: float32 [16], P('freq'), may hold values from 0.1 to 1
- cell_edges: int32 [12, 32768], P(None, 'dom'), may hold values from 0 to 4095
- log_cond: float32 [32768], P('dom'), may hold values from -6 to 6
Outputs:
- fwd_field: float32 [16, 4, 1024, 128], P('freq', None, 'dom')
- adj_field: float32 [16, 4, 1024, 128], P('freq', None, 'dom')
- model_next: float32 [32768], P('dom')
Inputs may be any that keep to these rules, and one draw needn't show every extreme that they name: `block_links`: entry 0 of each block row is the row's own local block; the others index the partition's extended field, local blocks first, then the tiles received in round 0, 1 and so on; every received tile is referenced by some row of the partition. `tile_lists`: the 16 blocks of one row are distinct local blocks.
All inputs are finite; a program needn't handle non-finite values.
Results may differ from a plain program's by a relative error of at most 0.0001.
Values sent between devices are 32-bit elements; how exact they have to be, the bound alone decides.
No kernel may reach another device: no remote copies, remote signals or barrier semaphores. Data moves between devices by JAX's collectives and lax.ppermute only.
A program may use at most 64 MiB of HBM per device.

v0:
```python
import jax
import jax.numpy as jnp
from jax import lax
from jax.sharding import PartitionSpec as P

ITERS = 3


def swapped(value, axis, distance):
    mask = 2**distance
    pairs = [(source, source ^ mask) for source in range(lax.axis_size(axis))]
    return lax.ppermute(value, axis, pairs)


def operate(field, curl_blocks, block_links, tile_lists, weight, trade):
    parts = [field]
    for bit in range(tile_lists.shape[0]):
        outgoing = jnp.take(field, tile_lists[bit], axis=0)
        parts.append(trade(outgoing, bit))
    extended = jnp.concatenate(parts, axis=0)
    shape = field.shape
    gathered = jnp.take(extended, block_links.reshape(-1), axis=0)
    gathered = gathered.reshape(block_links.shape + shape[1:])
    curl = jnp.einsum("blij,blmj->bmi", curl_blocks, gathered, precision=lax.Precision.HIGHEST)
    count = weight.shape[2]
    curl = curl.reshape(shape[0], -1, count, 2, 2, shape[2])
    split = field.reshape(shape[0], -1, count, 2, 2, shape[2])
    real_part = curl[:, :, :, :, 0] - weight * split[:, :, :, :, 1]
    imag_part = curl[:, :, :, :, 1] + weight * split[:, :, :, :, 0]
    return jnp.stack([real_part, imag_part], axis=4).reshape(shape)


def chebyshev(source, curl_blocks, block_links, tile_lists, weight, trade):
    theta = 1.0
    delta = 0.7
    sone = theta / delta
    rho = 1.0 / sone
    solution = jnp.zeros_like(source)
    resid = source
    direction = source / theta
    for step in range(ITERS):
        solution = solution + direction
        if step + 1 < ITERS:
            resid = resid - operate(direction, curl_blocks, block_links, tile_lists, weight, trade)
            rho_new = 1.0 / (2.0 * sone - rho)
            direction = rho_new * rho * direction + 2.0 * rho_new / delta * resid
            rho = rho_new
    return solution


def to_rows(fields):
    shape = fields.shape
    moved = jnp.transpose(fields, (3, 0, 1, 2, 4))
    return moved.reshape(shape[3], shape[0] * shape[1] * shape[2], shape[4])


def from_rows(rows, systems, count):
    shaped = rows.reshape(rows.shape[0], systems, count, 4, rows.shape[2])
    return jnp.transpose(shaped, (1, 2, 3, 0, 4))


def local(
    fwd_source,
    adj_source,
    curl_blocks,
    block_links,
    tile_lists,
    edge_mass,
    omega,
    cell_edges,
    log_cond,
):
    count = fwd_source.shape[0]
    weight = (edge_mass[:, None, :] * omega[None, :, None])[:, None, :, None, :]

    def trade_one(outgoing, bit):
        return swapped(outgoing, "dom", bit)

    fwd_rows = chebyshev(
        to_rows(fwd_source[None]), curl_blocks, block_links, tile_lists, weight, trade_one
    )
    adj_rows = chebyshev(
        to_rows(adj_source[None]), curl_blocks, block_links, tile_lists, weight, trade_one
    )
    efield = from_rows(fwd_rows, 1, count)[0]
    lfield = from_rows(adj_rows, 1, count)[0]
    edges = efield.shape[2] * efield.shape[3]
    esplit = efield.reshape(count, 2, 2, edges)
    lsplit = lfield.reshape(count, 2, 2, edges)
    prod = esplit[:, :, 0] * lsplit[:, :, 1] + esplit[:, :, 1] * lsplit[:, :, 0]
    edge_term = jnp.sum(omega[:, None, None] * prod, axis=(0, 1))
    picked = jnp.take(edge_term, cell_edges.reshape(-1), axis=0).reshape(cell_edges.shape)
    scale = 1.0 / jnp.sqrt(24.0 * count * lax.axis_size("freq"))
    partial_grad = jnp.sum(picked, axis=0) * scale
    grad = lax.psum(partial_grad, "freq")
    model_next = log_cond - 0.5 * grad / jnp.sqrt(grad * grad + 1.0)
    return (efield, lfield, model_next)


def solution(mesh):
    in_specs = (
        P("freq", None, "dom", None),
        P("freq", None, "dom", None),
        P("dom", None, None, None),
        P("dom", None),
        P("dom", None),
        P("dom", None),
        P("freq"),
        P(None, "dom"),
        P("dom"),
    )
    out_specs = (P("freq", None, "dom", None), P("freq", None, "dom", None), P("dom"))
    return jax.shard_map(local, mesh=mesh, in_specs=in_specs, out_specs=out_specs, check_vma=False)
```

profile of v0, /device:TPU:4, one launch (start us, length us, event | category | flops | bytes accessed | tf_op | source)
XLA Modules:
  0.0 182.5 jit_solution(15824569040240050575)
XLA Ops:
  0.6 0.8 compare_and_fusion.1
  1.5 1.0 copy.47
  2.5 1.0 copy.51
  3.5 0.6 gather_fusion.1
  4.1 0.6 gather_fusion.11
  4.8 0.6 gather_fusion.2
  5.4 0.6 gather_fusion.12
  6.1 2.0 %collective-permute-start.1 = (f32[16,8,128]{2,1,0:T(8,128)S(1)}, f32[16,8,128]{2,1,0:T(8,128)S(1)}, u32[]{:S(2)}, u32[]{:S(2)}) collective-permute-start(f32[16,8,128]{2,1,0:T(8,128)S(1)} %get-tuple-element.60), channel_id=1, source_target_pairs={{0,2},{1,3},{2,0},{3,1},{4,6},{5,7},{6,4},{7,5},{8,10},{9,11},{10,... | collective-permute-start | bytes 196616 | tf_op jit(solution)/shard_map/ppermute | solution.py:12
  8.1 0.6 gather_fusion.3
  8.7 0.6 gather_fusion.13
  9.3 3.4 %collective-permute-start.2 = (f32[16,8,128]{2,1,0:T(8,128)S(1)}, f32[16,8,128]{2,1,0:T(8,128)S(1)}, u32[]{:S(2)}, u32[]{:S(2)}) collective-permute-start(f32[16,8,128]{2,1,0:T(8,128)S(1)} %get-tuple-element.58), channel_id=1, source_target_pairs={{0,4},{1,5},{2,6},{3,7},{4,0},{5,1},{6,2},{7,3},{8,12},{9,13},{10,... | collective-permute-start | bytes 196616 | tf_op jit(solution)/shard_map/ppermute | solution.py:12
  12.7 0.6 gather_fusion.4
  13.3 0.6 gather_fusion.14
  13.9 1.3 collective-permute-start.3
  15.2 0.8 copy.46
  16.1 0.9 copy.60
  17.1 0.8 broadcast_multiply_fusion
  18.4 1.1 collective-permute-start.11
  19.5 0.8 gather_fusion.5
  20.3 3.4 %collective-permute-done.9 = f32[16,8,128]{2,1,0:T(8,128)S(1)} collective-permute-done((f32[16,8,128]{2,1,0:T(8,128)S(1)}, f32[16,8,128]{2,1,0:T(8,128)S(1)}, u32[]{:S(2)}, u32[]{:S(2)}) %collective-permute-start.9) | collective-permute-done | bytes 65568 | tf_op jit(solution)/shard_map/ppermute | solution.py:12
  23.7 1.3 collective-permute-done.10
  25.0 0.8 gather_fusion.15
  26.0 9.3 %convolution_bitcast_fusion.3 = f32[32,8,128]{2,1,0:T(8,128)S(1)} fusion(f32[32,4,8,128]{3,2,1,0:T(8,128)S(1)} %bitcast.106, f32[32,4,128,128]{3,2,1,0:T(8,128)} %param.15), kind=kOutput, calls=%fused_computation.24 | convolution fusion | flops 201326592 | bytes 9043968 | tf_op jit(solution)/shard_map/blij,blmj->bmi/dot_general | solution.py:24
  35.4 9.3 %convolution_bitcast_fusion.1 = f32[32,8,128]{2,1,0:T(8,128)S(1)} fusion(f32[32,4,8,128]{3,2,1,0:T(8,128)S(1)} %bitcast.104, f32[32,4,128,128]{3,2,1,0:T(8,128)} %param.15), kind=kOutput, calls=%fused_computation.22 | convolution fusion | flops 201326592 | bytes 9043968 | tf_op jit(solution)/shard_map/blij,blmj->bmi/dot_general | solution.py:24
  44.9 0.6 gather_fusion.6
  45.5 0.6 gather_fusion.7
  46.2 0.6 gather_fusion.16
  46.8 0.6 gather_fusion.17
  47.3 0.6 gather_fusion.8
  47.9 0.6 gather_fusion.18
  48.5 0.6 gather_fusion.9
  49.1 0.6 gather_fusion.19
  49.9 0.4 collective-permute-start.5
  50.4 2.3 %collective-permute-start.6 = (f32[16,8,128]{2,1,0:T(8,128)S(1)}, f32[16,8,128]{2,1,0:T(8,128)S(1)}, u32[]{:S(2)}, u32[]{:S(2)}) collective-permute-start(f32[16,8,128]{2,1,0:T(8,128)S(1)} %get-tuple-element.48), channel_id=1, source_target_pairs={{0,4},{1,5},{2,6},{3,7},{4,0},{5,1},{6,2},{7,3},{8,12},{9,13},{10,... | collective-permute-start | bytes 196616 | tf_op jit(solution)/shard_map/ppermute | solution.py:12
  52.8 0.9 collective-permute-start.7
  53.8 1.2 collective-permute-start.15
  55.0 0.7 collective-permute-start.14
  55.7 1.8 collective-permute-start.13
  57.8 0.8 gather_fusion.10
  59.0 1.7 collective-permute-done.13
  60.8 0.8 gather_fusion.20
  61.8 9.3 %convolution_bitcast_fusion.2 = f32[32,8,128]{2,1,0:T(8,128)S(1)} fusion(f32[32,4,8,128]{3,2,1,0:T(8,128)S(1)} %bitcast.105, f32[32,4,128,128]{3,2,1,0:T(8,128)} %param.15), kind=kOutput, calls=%fused_computation.23 | convolution fusion | flops 201326592 | bytes 9043968 | tf_op jit(solution)/shard_map/blij,blmj->bmi/dot_general | solution.py:24
  71.1 9.3 %convolution_bitcast_fusion = f32[32,8,128]{2,1,0:T(8,128)S(1)} fusion(f32[32,4,8,128]{3,2,1,0:T(8,128)S(1)} %bitcast.103, f32[32,4,128,128]{3,2,1,0:T(8,128)} %param.15), kind=kOutput, calls=%fused_computation.21 | convolution fusion | flops 201326592 | bytes 9043968 | tf_op jit(solution)/shard_map/blij,blmj->bmi/dot_general | solution.py:24
  80.4 0.7 fusion.17
  81.2 0.7 fusion.15
  82.3 68.0 %gather_fusion = f32[12288]{0:T(1024)S(1)} fusion(f32[4096]{0:T(1024)S(1)} %fusion.13, s32[12288]{0:T(1024)S(1)} %broadcast_clamp_fusion), kind=kCustom, calls=%fused_computation.20 | custom fusion | bytes 147456 | tf_op jit(solution)/shard_map/jit(_take)/gather | solution.py:92
  150.5 31.5 %psum.7 = f32[1024]{0:T(1024)S(1)} all-reduce(f32[1024]{0:T(1024)S(1)} %broadcast_multiply_fusion.1), channel_id=1, replica_groups=mesh['freq'=8,'dom'=32] {'freq'}, use_global_device_ids=true, to_apply=%region_2.5 | all-reduce | flops 1024 | bytes 8192 | tf_op jit(solution)/shard_map/psum | solution.py:95
  181.9 0.6 multiply_subtract_fusion
  (85 shorter events, 3.8 us)
Async XLA Ops:
  4.7 13.2 %collective-permute-start = (f32[16,8,128]{2,1,0:T(8,128)S(1)}, f32[16,8,128]{2,1,0:T(8,128)S(1)}, u32[]{:S(2)}, u32[]{:S(2)}) collective-permute-start(f32[16,8,128]{2,1,0:T(8,128)S(1)} %get-tuple-element.62), channel_id=1, source_target_pairs={{0,1},{1,0},{2,3},{3,2},{4,5},{5,4},{6,7},{7,6},{8,9},{9,8},{10,11... | collective-permute-start | bytes 196616 | tf_op jit(solution)/shard_map/ppermute | solution.py:12
  6.1 12.1 %collective-permute-start.1 = (f32[16,8,128]{2,1,0:T(8,128)S(1)}, f32[16,8,128]{2,1,0:T(8,128)S(1)}, u32[]{:S(2)}, u32[]{:S(2)}) collective-permute-start(f32[16,8,128]{2,1,0:T(8,128)S(1)} %get-tuple-element.60), channel_id=1, source_target_pairs={{0,2},{1,3},{2,0},{3,1},{4,6},{5,7},{6,4},{7,5},{8,10},{9,11},{10,... | collective-permute-start | bytes 196616 | tf_op jit(solution)/shard_map/ppermute | solution.py:12
  9.3 9.1 %collective-permute-start.2 = (f32[16,8,128]{2,1,0:T(8,128)S(1)}, f32[16,8,128]{2,1,0:T(8,128)S(1)}, u32[]{:S(2)}, u32[]{:S(2)}) collective-permute-start(f32[16,8,128]{2,1,0:T(8,128)S(1)} %get-tuple-element.58), channel_id=1, source_target_pairs={{0,4},{1,5},{2,6},{3,7},{4,0},{5,1},{6,2},{7,3},{8,12},{9,13},{10,... | collective-permute-start | bytes 196616 | tf_op jit(solution)/shard_map/ppermute | solution.py:12
  13.9 5.6 %collective-permute-start.3 = (f32[16,8,128]{2,1,0:T(8,128)S(1)}, f32[16,8,128]{2,1,0:T(8,128)S(1)}, u32[]{:S(2)}, u32[]{:S(2)}) collective-permute-start(f32[16,8,128]{2,1,0:T(8,128)S(1)} %get-tuple-element.56), channel_id=1, source_target_pairs={{0,8},{1,9},{2,10},{3,11},{4,12},{5,13},{6,14},{7,15},{8,0},{9,1},... | collective-permute-start | bytes 196616 | tf_op jit(solution)/shard_map/ppermute | solution.py:12
  15.2 5.1 %collective-permute-start.8 = (f32[16,8,128]{2,1,0:T(8,128)S(1)}, f32[16,8,128]{2,1,0:T(8,128)S(1)}, u32[]{:S(2)}, u32[]{:S(2)}) collective-permute-start(f32[16,8,128]{2,1,0:T(8,128)S(1)} %get-tuple-element.61), channel_id=1, source_target_pairs={{0,1},{1,0},{2,3},{3,2},{4,5},{5,4},{6,7},{7,6},{8,9},{9,8},{10,11... | collective-permute-start | bytes 196616 | tf_op jit(solution)/shard_map/ppermute | solution.py:12
  17.9 5.8 %collective-permute-start.9 = (f32[16,8,128]{2,1,0:T(8,128)S(1)}, f32[16,8,128]{2,1,0:T(8,128)S(1)}, u32[]{:S(2)}, u32[]{:S(2)}) collective-permute-start(f32[16,8,128]{2,1,0:T(8,128)S(1)} %get-tuple-element.59), channel_id=1, source_target_pairs={{0,2},{1,3},{2,0},{3,1},{4,6},{5,7},{6,4},{7,5},{8,10},{9,11},{10,... | collective-permute-start | bytes 196616 | tf_op jit(solution)/shard_map/ppermute | solution.py:12
  18.1 6.9 %collective-permute-start.10 = (f32[16,8,128]{2,1,0:T(8,128)S(1)}, f32[16,8,128]{2,1,0:T(8,128)S(1)}, u32[]{:S(2)}, u32[]{:S(2)}) collective-permute-start(f32[16,8,128]{2,1,0:T(8,128)S(1)} %get-tuple-element.57), channel_id=1, source_target_pairs={{0,4},{1,5},{2,6},{3,7},{4,0},{5,1},{6,2},{7,3},{8,12},{9,13},{10,... | collective-permute-start | bytes 196616 | tf_op jit(solution)/shard_map/ppermute | solution.py:12
  18.4 6.6 %collective-permute-start.11 = (f32[16,8,128]{2,1,0:T(8,128)S(1)}, f32[16,8,128]{2,1,0:T(8,128)S(1)}, u32[]{:S(2)}, u32[]{:S(2)}) collective-permute-start(f32[16,8,128]{2,1,0:T(8,128)S(1)} %get-tuple-element.55), channel_id=1, source_target_pairs={{0,8},{1,9},{2,10},{3,11},{4,12},{5,13},{6,14},{7,15},{8,0},{9,1},... | collective-permute-start | bytes 196616 | tf_op jit(solution)/shard_map/ppermute | solution.py:12
  26.0 18.7 %copy-start = (f32[2,4,32,128]{3,2,1,0:T(8,128)S(1)}, f32[2,4,32,128]{3,2,1,0:T(8,128)}, u32[]{:S(2)}) copy-start(f32[2,4,32,128]{3,2,1,0:T(8,128)} %param.14) | copy-start | bytes 393220
  26.0 18.7 %copy-start.1 = (f32[2,4,32,128]{3,2,1,0:T(8,128)S(1)}, f32[2,4,32,128]{3,2,1,0:T(8,128)}, u32[]{:S(2)}) copy-start(f32[2,4,32,128]{3,2,1,0:T(8,128)} %param.13) | copy-start | bytes 393220
  49.7 5.2 %collective-permute-start.4 = (f32[16,8,128]{2,1,0:T(8,128)S(1)}, f32[16,8,128]{2,1,0:T(8,128)S(1)}, u32[]{:S(2)}, u32[]{:S(2)}) collective-permute-start(f32[16,8,128]{2,1,0:T(8,128)S(1)} %get-tuple-element.52), channel_id=1, source_target_pairs={{0,1},{1,0},{2,3},{3,2},{4,5},{5,4},{6,7},{7,6},{8,9},{9,8},{10,11... | collective-permute-start | bytes 196616 | tf_op jit(solution)/shard_map/ppermute | solution.py:12
  49.9 5.8 %collective-permute-start.5 = (f32[16,8,128]{2,1,0:T(8,128)S(1)}, f32[16,8,128]{2,1,0:T(8,128)S(1)}, u32[]{:S(2)}, u32[]{:S(2)}) collective-permute-start(f32[16,8,128]{2,1,0:T(8,128)S(1)} %get-tuple-element.50), channel_id=1, source_target_pairs={{0,2},{1,3},{2,0},{3,1},{4,6},{5,7},{6,4},{7,5},{8,10},{9,11},{10,... | collective-permute-start | bytes 196616 | tf_op jit(solution)/shard_map/ppermute | solution.py:12
  50.4 7.0 %collective-permute-start.6 = (f32[16,8,128]{2,1,0:T(8,128)S(1)}, f32[16,8,128]{2,1,0:T(8,128)S(1)}, u32[]{:S(2)}, u32[]{:S(2)}) collective-permute-start(f32[16,8,128]{2,1,0:T(8,128)S(1)} %get-tuple-element.48), channel_id=1, source_target_pairs={{0,4},{1,5},{2,6},{3,7},{4,0},{5,1},{6,2},{7,3},{8,12},{9,13},{10,... | collective-permute-start | bytes 196616 | tf_op jit(solution)/shard_map/ppermute | solution.py:12
  52.8 4.9 %collective-permute-start.7 = (f32[16,8,128]{2,1,0:T(8,128)S(1)}, f32[16,8,128]{2,1,0:T(8,128)S(1)}, u32[]{:S(2)}, u32[]{:S(2)}) collective-permute-start(f32[16,8,128]{2,1,0:T(8,128)S(1)} %get-tuple-element.46), channel_id=1, source_target_pairs={{0,8},{1,9},{2,10},{3,11},{4,12},{5,13},{6,14},{7,15},{8,0},{9,1},... | collective-permute-start | bytes 196616 | tf_op jit(solution)/shard_map/ppermute | solution.py:12
  53.8 7.0 %collective-permute-start.15 = (f32[16,8,128]{2,1,0:T(8,128)S(1)}, f32[16,8,128]{2,1,0:T(8,128)S(1)}, u32[]{:S(2)}, u32[]{:S(2)}) collective-permute-start(f32[16,8,128]{2,1,0:T(8,128)S(1)} %get-tuple-element.45), channel_id=1, source_target_pairs={{0,8},{1,9},{2,10},{3,11},{4,12},{5,13},{6,14},{7,15},{8,0},{9,1},... | collective-permute-start | bytes 196616 | tf_op jit(solution)/shard_map/ppermute | solution.py:12
  55.0 5.8 %collective-permute-start.14 = (f32[16,8,128]{2,1,0:T(8,128)S(1)}, f32[16,8,128]{2,1,0:T(8,128)S(1)}, u32[]{:S(2)}, u32[]{:S(2)}) collective-permute-start(f32[16,8,128]{2,1,0:T(8,128)S(1)} %get-tuple-element.47), channel_id=1, source_target_pairs={{0,4},{1,5},{2,6},{3,7},{4,0},{5,1},{6,2},{7,3},{8,12},{9,13},{10,... | collective-permute-start | bytes 196616 | tf_op jit(solution)/shard_map/ppermute | solution.py:12
  55.7 5.1 %collective-permute-start.13 = (f32[16,8,128]{2,1,0:T(8,128)S(1)}, f32[16,8,128]{2,1,0:T(8,128)S(1)}, u32[]{:S(2)}, u32[]{:S(2)}) collective-permute-start(f32[16,8,128]{2,1,0:T(8,128)S(1)} %get-tuple-element.49), channel_id=1, source_target_pairs={{0,2},{1,3},{2,0},{3,1},{4,6},{5,7},{6,4},{7,5},{8,10},{9,11},{10,... | collective-permute-start | bytes 196616 | tf_op jit(solution)/shard_map/ppermute | solution.py:12
  57.4 1.6 collective-permute-start.12
  71.0 11.1 %copy-start.4 = (f32[2]{0:T(128)S(1)}, f32[2]{0:T(128)}, u32[]{:S(2)}) copy-start(f32[2]{0:T(128)} %param.19) | copy-start | bytes 28
  82.3 68.1 %copy-start.2 = (s32[12,1024]{1,0:T(8,128)S(1)}, s32[12,1024]{1,0:T(8,128)}, u32[]{:S(2)}) copy-start(s32[12,1024]{1,0:T(8,128)} %param.20) | copy-start | bytes 147460
  82.3 99.6 %copy-start.3 = (f32[1024]{0:T(1024)S(1)}, f32[1024]{0:T(1024)}, u32[]{:S(2)}) copy-start(f32[1024]{0:T(1024)} %param.21) | copy-start | bytes 12292
where the time goes:
time: 183 us
  local copies, waits for them, and re-layouts  84.3 us (46%)
  matrix products  37 us (20%)
  blocking collectives  31.5 us (17%)
  starting transfers between devices  16 us (9%)
  waiting for transfers between devices  6.85 us (4%)
  other arithmetic  5.52 us (3%)
    gather x2, local copies, waits for them, and re-layouts, local(): jnp.take(edge_term, cell_edges.reshape(-1), axis=0)  68 us
    dot_general x4, matrix products, operate(): jnp.einsum('blij,blmj->bmi', curl_blocks, gathered, precision=lax.Precisi...  37 us
    psum x1, blocking collectives, local(): grad = lax.psum(partial_grad, 'freq')  31.5 us
    ppermute x16, starting transfers between devices, swapped(): return lax.ppermute(value, axis, pairs)  16 us
    gather x16, local copies, waits for them, and re-layouts, operate(): outgoing = jnp.take(field, tile_lists[bit], axis=0)  9.04 us
    ppermute x16, waiting for transfers between devices, swapped(): return lax.ppermute(value, axis, pairs)  6.85 us
  transfers between devices with their start and end apart: 16, of which 4 were waited for; matrix products, arithmetic and copies ran while one was open for 4% of the time, Pallas kernels for 0%

commit v1 on v0

--- a/solution.py
+++ b/solution.py
@@ -4,6 +4,10 @@
 from jax.sharding import PartitionSpec as P
 
 ITERS = 3
+
+
+def _direct_task(inner_x, lane_axis):
+    return lax.all_gather(inner_x, lane_axis).sum(axis=0)
 
 
 def swapped(value, axis, distance):
@@ -92,7 +96,7 @@
     picked = jnp.take(edge_term, cell_edges.reshape(-1), axis=0).reshape(cell_edges.shape)
     scale = 1.0 / jnp.sqrt(24.0 * count * lax.axis_size("freq"))
     partial_grad = jnp.sum(picked, axis=0) * scale
-    grad = lax.psum(partial_grad, "freq")
+    grad = _direct_task(partial_grad, "freq")
     model_next = log_cond - 0.5 * grad / jnp.sqrt(grad * grad + 1.0)
     return (efield, lfield, model_next)
 

time: 183 us -> 195 us (1.066)
  blocking collectives: 31.5 us -> 44.1 us
    all_gather x0 -> x1, blocking collectives: none -> 44.1 us  [_direct_task(): return lax.all_gather(inner_x, lane_axis).sum(axis=0)]
    psum x1 -> x0, blocking collectives: 31.5 us -> none  [local(): grad = lax.psum(partial_grad, 'freq')]
where the time goes in v1:
time: 195 us
  local copies, waits for them, and re-layouts  84.3 us (43%)
  blocking collectives  44.1 us (23%)
  matrix products  37 us (19%)
  starting transfers between devices  16 us (8%)
  waiting for transfers between devices  6.85 us (4%)
  other arithmetic  5.54 us (3%)
    gather x2, local copies, waits for them, and re-layouts, local(): jnp.take(edge_term, cell_edges.reshape(-1), axis=0)  68 us
    all_gather x1, blocking collectives, _direct_task(): return lax.all_gather(inner_x, lane_axis).sum(axis=0)  44.1 us
    dot_general x4, matrix products, operate(): jnp.einsum('blij,blmj->bmi', curl_blocks, gathered, precision=lax.Precisi...  37 us
    ppermute x16, starting transfers between devices, swapped(): return lax.ppermute(value, axis, pairs)  16 us
    gather x16, local copies, waits for them, and re-layouts, operate(): outgoing = jnp.take(field, tile_lists[bit], axis=0)  9.04 us
    ppermute x16, waiting for transfers between devices, swapped(): return lax.ppermute(value, axis, pairs)  6.85 us
  transfers between devices with their start and end apart: 16, of which 4 were waited for; matrix products, arithmetic and copies ran while one was open for 4% of the time, Pallas kernels for 0%

profile of v1, /device:TPU:4, one launch (start us, length us, event | category | flops | bytes accessed | tf_op | source)
XLA Modules:
  0.0 195.2 jit_solution(3155854951451693965)
XLA Ops:
  0.6 0.8 compare_and_fusion.1
  1.5 1.0 copy.77
  2.5 1.0 copy.81
  3.5 0.6 gather_fusion.1
  4.1 0.6 gather_fusion.11
  4.8 0.6 gather_fusion.2
  5.4 0.6 gather_fusion.12
  6.1 2.0 %collective-permute-start.1 = (f32[16,8,128]{2,1,0:T(8,128)S(1)}, f32[16,8,128]{2,1,0:T(8,128)S(1)}, u32[]{:S(2)}, u32[]{:S(2)}) collective-permute-start(f32[16,8,128]{2,1,0:T(8,128)S(1)} %get-tuple-element.60), channel_id=1, source_target_pairs={{0,2},{1,3},{2,0},{3,1},{4,6},{5,7},{6,4},{7,5},{8,10},{9,11},{10,... | collective-permute-start | bytes 196616 | tf_op jit(solution)/shard_map/ppermute | solution.py:16
  8.1 0.6 gather_fusion.3
  8.7 0.6 gather_fusion.13
  9.3 3.4 %collective-permute-start.2 = (f32[16,8,128]{2,1,0:T(8,128)S(1)}, f32[16,8,128]{2,1,0:T(8,128)S(1)}, u32[]{:S(2)}, u32[]{:S(2)}) collective-permute-start(f32[16,8,128]{2,1,0:T(8,128)S(1)} %get-tuple-element.58), channel_id=1, source_target_pairs={{0,4},{1,5},{2,6},{3,7},{4,0},{5,1},{6,2},{7,3},{8,12},{9,13},{10,... | collective-permute-start | bytes 196616 | tf_op jit(solution)/shard_map/ppermute | solution.py:16
  12.7 0.6 gather_fusion.4
  13.3 0.6 gather_fusion.14
  13.9 1.3 collective-permute-start.3
  15.2 0.8 copy.76
  16.1 0.9 copy.90
  17.1 0.8 broadcast_multiply_fusion
  18.4 1.1 collective-permute-start.11
  19.5 0.8 gather_fusion.5
  20.3 3.4 %collective-permute-done.9 = f32[16,8,128]{2,1,0:T(8,128)S(1)} collective-permute-done((f32[16,8,128]{2,1,0:T(8,128)S(1)}, f32[16,8,128]{2,1,0:T(8,128)S(1)}, u32[]{:S(2)}, u32[]{:S(2)}) %collective-permute-start.9) | collective-permute-done | bytes 65568 | tf_op jit(solution)/shard_map/ppermute | solution.py:16
  23.7 1.3 collective-permute-done.10
  25.0 0.8 gather_fusion.15
  26.0 9.3 %convolution_bitcast_fusion.3 = f32[32,8,128]{2,1,0:T(8,128)S(1)} fusion(f32[32,4,8,128]{3,2,1,0:T(8,128)S(1)} %bitcast.106, f32[32,4,128,128]{3,2,1,0:T(8,128)} %param.15), kind=kOutput, calls=%fused_computation.24 | convolution fusion | flops 201326592 | bytes 9043968 | tf_op jit(solution)/shard_map/blij,blmj->bmi/dot_general | solution.py:28
  35.4 9.3 %convolution_bitcast_fusion.1 = f32[32,8,128]{2,1,0:T(8,128)S(1)} fusion(f32[32,4,8,128]{3,2,1,0:T(8,128)S(1)} %bitcast.104, f32[32,4,128,128]{3,2,1,0:T(8,128)} %param.15), kind=kOutput, calls=%fused_computation.22 | convolution fusion | flops 201326592 | bytes 9043968 | tf_op jit(solution)/shard_map/blij,blmj->bmi/dot_general | solution.py:28
  44.9 0.6 gather_fusion.6
  45.5 0.6 gather_fusion.7
  46.2 0.6 gather_fusion.16
  46.8 0.6 gather_fusion.17
  47.3 0.6 gather_fusion.8
  47.9 0.6 gather_fusion.18
  48.5 0.6 gather_fusion.9
  49.1 0.6 gather_fusion.19
  49.9 0.4 collective-permute-start.5
  50.4 2.3 %collective-permute-start.6 = (f32[16,8,128]{2,1,0:T(8,128)S(1)}, f32[16,8,128]{2,1,0:T(8,128)S(1)}, u32[]{:S(2)}, u32[]{:S(2)}) collective-permute-start(f32[16,8,128]{2,1,0:T(8,128)S(1)} %get-tuple-element.48), channel_id=1, source_target_pairs={{0,4},{1,5},{2,6},{3,7},{4,0},{5,1},{6,2},{7,3},{8,12},{9,13},{10,... | collective-permute-start | bytes 196616 | tf_op jit(solution)/shard_map/ppermute | solution.py:16
  52.8 0.9 collective-permute-start.7
  53.8 1.2 collective-permute-start.15
  55.0 0.7 collective-permute-start.14
  55.7 1.8 collective-permute-start.13
  57.8 0.8 gather_fusion.10
  59.0 1.7 collective-permute-done.13
  60.8 0.8 gather_fusion.20
  61.8 9.3 %convolution_bitcast_fusion.2 = f32[32,8,128]{2,1,0:T(8,128)S(1)} fusion(f32[32,4,8,128]{3,2,1,0:T(8,128)S(1)} %bitcast.105, f32[32,4,128,128]{3,2,1,0:T(8,128)} %param.15), kind=kOutput, calls=%fused_computation.23 | convolution fusion | flops 201326592 | bytes 9043968 | tf_op jit(solution)/shard_map/blij,blmj->bmi/dot_general | solution.py:28
  71.1 9.3 %convolution_bitcast_fusion = f32[32,8,128]{2,1,0:T(8,128)S(1)} fusion(f32[32,4,8,128]{3,2,1,0:T(8,128)S(1)} %bitcast.103, f32[32,4,128,128]{3,2,1,0:T(8,128)} %param.15), kind=kOutput, calls=%fused_computation.21 | convolution fusion | flops 201326592 | bytes 9043968 | tf_op jit(solution)/shard_map/blij,blmj->bmi/dot_general | solution.py:28
  80.4 0.7 fusion.17
  81.2 0.7 fusion.15
  82.3 68.0 %gather_fusion = f32[12288]{0:T(1024)S(1)} fusion(f32[4096]{0:T(1024)S(1)} %fusion.13, s32[12288]{0:T(1024)S(1)} %broadcast_clamp_fusion), kind=kCustom, calls=%fused_computation.20 | custom fusion | bytes 147456 | tf_op jit(solution)/shard_map/jit(_take)/gather | solution.py:96
  150.5 44.1 %all-gather = f32[8192]{0:T(1024)S(1)} all-gather(f32[1024]{0:T(1024)S(1)} %broadcast_multiply_fusion.1), channel_id=2, replica_groups=mesh['freq'=8,'dom'=32] {'freq'}, dimensions={0}, use_global_device_ids=true | all-gather | bytes 36864 | tf_op jit(solution)/shard_map/all_gather | solution.py:10
  194.6 0.6 multiply_subtract_fusion
  (87 shorter events, 3.9 us)
Async XLA Ops:
  4.7 13.2 %collective-permute-start = (f32[16,8,128]{2,1,0:T(8,128)S(1)}, f32[16,8,128]{2,1,0:T(8,128)S(1)}, u32[]{:S(2)}, u32[]{:S(2)}) collective-permute-start(f32[16,8,128]{2,1,0:T(8,128)S(1)} %get-tuple-element.62), channel_id=1, source_target_pairs={{0,1},{1,0},{2,3},{3,2},{4,5},{5,4},{6,7},{7,6},{8,9},{9,8},{10,11... | collective-permute-start | bytes 196616 | tf_op jit(solution)/shard_map/ppermute | solution.py:16
  6.1 12.1 %collective-permute-start.1 = (f32[16,8,128]{2,1,0:T(8,128)S(1)}, f32[16,8,128]{2,1,0:T(8,128)S(1)}, u32[]{:S(2)}, u32[]{:S(2)}) collective-permute-start(f32[16,8,128]{2,1,0:T(8,128)S(1)} %get-tuple-element.60), channel_id=1, source_target_pairs={{0,2},{1,3},{2,0},{3,1},{4,6},{5,7},{6,4},{7,5},{8,10},{9,11},{10,... | collective-permute-start | bytes 196616 | tf_op jit(solution)/shard_map/ppermute | solution.py:16
  9.3 9.1 %collective-permute-start.2 = (f32[16,8,128]{2,1,0:T(8,128)S(1)}, f32[16,8,128]{2,1,0:T(8,128)S(1)}, u32[]{:S(2)}, u32[]{:S(2)}) collective-permute-start(f32[16,8,128]{2,1,0:T(8,128)S(1)} %get-tuple-element.58), channel_id=1, source_target_pairs={{0,4},{1,5},{2,6},{3,7},{4,0},{5,1},{6,2},{7,3},{8,12},{9,13},{10,... | collective-permute-start | bytes 196616 | tf_op jit(solution)/shard_map/ppermute | solution.py:16
  13.9 5.6 %collective-permute-start.3 = (f32[16,8,128]{2,1,0:T(8,128)S(1)}, f32[16,8,128]{2,1,0:T(8,128)S(1)}, u32[]{:S(2)}, u32[]{:S(2)}) collective-permute-start(f32[16,8,128]{2,1,0:T(8,128)S(1)} %get-tuple-element.56), channel_id=1, source_target_pairs={{0,8},{1,9},{2,10},{3,11},{4,12},{5,13},{6,14},{7,15},{8,0},{9,1},... | collective-permute-start | bytes 196616 | tf_op jit(solution)/shard_map/ppermute | solution.py:16
  15.2 5.1 %collective-permute-start.8 = (f32[16,8,128]{2,1,0:T(8,128)S(1)}, f32[16,8,128]{2,1,0:T(8,128)S(1)}, u32[]{:S(2)}, u32[]{:S(2)}) collective-permute-start(f32[16,8,128]{2,1,0:T(8,128)S(1)} %get-tuple-element.61), channel_id=1, source_target_pairs={{0,1},{1,0},{2,3},{3,2},{4,5},{5,4},{6,7},{7,6},{8,9},{9,8},{10,11... | collective-permute-start | bytes 196616 | tf_op jit(solution)/shard_map/ppermute | solution.py:16
  17.9 5.8 %collective-permute-start.9 = (f32[16,8,128]{2,1,0:T(8,128)S(1)}, f32[16,8,128]{2,1,0:T(8,128)S(1)}, u32[]{:S(2)}, u32[]{:S(2)}) collective-permute-start(f32[16,8,128]{2,1,0:T(8,128)S(1)} %get-tuple-element.59), channel_id=1, source_target_pairs={{0,2},{1,3},{2,0},{3,1},{4,6},{5,7},{6,4},{7,5},{8,10},{9,11},{10,... | collective-permute-start | bytes 196616 | tf_op jit(solution)/shard_map/ppermute | solution.py:16
  18.1 6.9 %collective-permute-start.10 = (f32[16,8,128]{2,1,0:T(8,128)S(1)}, f32[16,8,128]{2,1,0:T(8,128)S(1)}, u32[]{:S(2)}, u32[]{:S(2)}) collective-permute-start(f32[16,8,128]{2,1,0:T(8,128)S(1)} %get-tuple-element.57), channel_id=1, source_target_pairs={{0,4},{1,5},{2,6},{3,7},{4,0},{5,1},{6,2},{7,3},{8,12},{9,13},{10,... | collective-permute-start | bytes 196616 | tf_op jit(solution)/shard_map/ppermute | solution.py:16
  18.4 6.6 %collective-permute-start.11 = (f32[16,8,128]{2,1,0:T(8,128)S(1)}, f32[16,8,128]{2,1,0:T(8,128)S(1)}, u32[]{:S(2)}, u32[]{:S(2)}) collective-permute-start(f32[16,8,128]{2,1,0:T(8,128)S(1)} %get-tuple-element.55), channel_id=1, source_target_pairs={{0,8},{1,9},{2,10},{3,11},{4,12},{5,13},{6,14},{7,15},{8,0},{9,1},... | collective-permute-start | bytes 196616 | tf_op jit(solution)/shard_map/ppermute | solution.py:16
  26.0 18.7 %copy-start = (f32[2,4,32,128]{3,2,1,0:T(8,128)S(1)}, f32[2,4,32,128]{3,2,1,0:T(8,128)}, u32[]{:S(2)}) copy-start(f32[2,4,32,128]{3,2,1,0:T(8,128)} %param.14) | copy-start | bytes 393220
  26.0 18.7 %copy-start.1 = (f32[2,4,32,128]{3,2,1,0:T(8,128)S(1)}, f32[2,4,32,128]{3,2,1,0:T(8,128)}, u32[]{:S(2)}) copy-start(f32[2,4,32,128]{3,2,1,0:T(8,128)} %param.13) | copy-start | bytes 393220
  49.7 5.2 %collective-permute-start.4 = (f32[16,8,128]{2,1,0:T(8,128)S(1)}, f32[16,8,128]{2,1,0:T(8,128)S(1)}, u32[]{:S(2)}, u32[]{:S(2)}) collective-permute-start(f32[16,8,128]{2,1,0:T(8,128)S(1)} %get-tuple-element.52), channel_id=1, source_target_pairs={{0,1},{1,0},{2,3},{3,2},{4,5},{5,4},{6,7},{7,6},{8,9},{9,8},{10,11... | collective-permute-start | bytes 196616 | tf_op jit(solution)/shard_map/ppermute | solution.py:16
  49.9 5.8 %collective-permute-start.5 = (f32[16,8,128]{2,1,0:T(8,128)S(1)}, f32[16,8,128]{2,1,0:T(8,128)S(1)}, u32[]{:S(2)}, u32[]{:S(2)}) collective-permute-start(f32[16,8,128]{2,1,0:T(8,128)S(1)} %get-tuple-element.50), channel_id=1, source_target_pairs={{0,2},{1,3},{2,0},{3,1},{4,6},{5,7},{6,4},{7,5},{8,10},{9,11},{10,... | collective-permute-start | bytes 196616 | tf_op jit(solution)/shard_map/ppermute | solution.py:16
  50.4 7.0 %collective-permute-start.6 = (f32[16,8,128]{2,1,0:T(8,128)S(1)}, f32[16,8,128]{2,1,0:T(8,128)S(1)}, u32[]{:S(2)}, u32[]{:S(2)}) collective-permute-start(f32[16,8,128]{2,1,0:T(8,128)S(1)} %get-tuple-element.48), channel_id=1, source_target_pairs={{0,4},{1,5},{2,6},{3,7},{4,0},{5,1},{6,2},{7,3},{8,12},{9,13},{10,... | collective-permute-start | bytes 196616 | tf_op jit(solution)/shard_map/ppermute | solution.py:16
  52.8 4.9 %collective-permute-start.7 = (f32[16,8,128]{2,1,0:T(8,128)S(1)}, f32[16,8,128]{2,1,0:T(8,128)S(1)}, u32[]{:S(2)}, u32[]{:S(2)}) collective-permute-start(f32[16,8,128]{2,1,0:T(8,128)S(1)} %get-tuple-element.46), channel_id=1, source_target_pairs={{0,8},{1,9},{2,10},{3,11},{4,12},{5,13},{6,14},{7,15},{8,0},{9,1},... | collective-permute-start | bytes 196616 | tf_op jit(solution)/shard_map/ppermute | solution.py:16
  53.8 7.0 %collective-permute-start.15 = (f32[16,8,128]{2,1,0:T(8,128)S(1)}, f32[16,8,128]{2,1,0:T(8,128)S(1)}, u32[]{:S(2)}, u32[]{:S(2)}) collective-permute-start(f32[16,8,128]{2,1,0:T(8,128)S(1)} %get-tuple-element.45), channel_id=1, source_target_pairs={{0,8},{1,9},{2,10},{3,11},{4,12},{5,13},{6,14},{7,15},{8,0},{9,1},... | collective-permute-start | bytes 196616 | tf_op jit(solution)/shard_map/ppermute | solution.py:16
  55.0 5.8 %collective-permute-start.14 = (f32[16,8,128]{2,1,0:T(8,128)S(1)}, f32[16,8,128]{2,1,0:T(8,128)S(1)}, u32[]{:S(2)}, u32[]{:S(2)}) collective-permute-start(f32[16,8,128]{2,1,0:T(8,128)S(1)} %get-tuple-element.47), channel_id=1, source_target_pairs={{0,4},{1,5},{2,6},{3,7},{4,0},{5,1},{6,2},{7,3},{8,12},{9,13},{10,... | collective-permute-start | bytes 196616 | tf_op jit(solution)/shard_map/ppermute | solution.py:16
  55.7 5.1 %collective-permute-start.13 = (f32[16,8,128]{2,1,0:T(8,128)S(1)}, f32[16,8,128]{2,1,0:T(8,128)S(1)}, u32[]{:S(2)}, u32[]{:S(2)}) collective-permute-start(f32[16,8,128]{2,1,0:T(8,128)S(1)} %get-tuple-element.49), channel_id=1, source_target_pairs={{0,2},{1,3},{2,0},{3,1},{4,6},{5,7},{6,4},{7,5},{8,10},{9,11},{10,... | collective-permute-start | bytes 196616 | tf_op jit(solution)/shard_map/ppermute | solution.py:16
  57.4 1.6 collective-permute-start.12
  71.0 11.1 %copy-start.4 = (f32[2]{0:T(128)S(1)}, f32[2]{0:T(128)}, u32[]{:S(2)}) copy-start(f32[2]{0:T(128)} %param.19) | copy-start | bytes 28
  82.3 68.1 %copy-start.2 = (s32[12,1024]{1,0:T(8,128)S(1)}, s32[12,1024]{1,0:T(8,128)}, u32[]{:S(2)}) copy-start(s32[12,1024]{1,0:T(8,128)} %param.20) | copy-start | bytes 147460
  82.3 112.2 %copy-start.3 = (f32[1024]{0:T(1024)S(1)}, f32[1024]{0:T(1024)}, u32[]{:S(2)}) copy-start(f32[1024]{0:T(1024)} %param.21) | copy-start | bytes 12292
